TPU v7x, 32 devices: a whole 2x2x4 slice. The times are simulated.
32 devices in a mesh: clips: 2 (over x), seq: 8 (over z, y), head: 2 (over core).
Axes of the slice: x: 2, y: 2, z: 4, core: 2. Of those that a mesh axis runs over, the one named last changes fastest.
Arguments:
- video_q: bfloat16 [2048, 2048], P(('clips', 'seq'), 'head'), parts along dimension 0, may hold values from -105 to 105
- video_k: bfloat16 [2048, 2048], P(('clips', 'seq'), 'head'), parts along dimension 0, may hold values from -5 to 5
- video_v: bfloat16 [2048, 2048], P(('clips', 'seq'), 'head'), parts along dimension 0, may hold values from -6 to 6
- audio_q: bfloat16 [512, 2048], P(('clips', 'seq'), 'head'), parts along dimension 0, may hold values from -105 to 105
- audio_k: bfloat16 [512, 2048], P(('clips', 'seq'), 'head'), parts along dimension 0, may hold values from -5 to 5
- audio_v: bfloat16 [512, 2048], P(('clips', 'seq'), 'head'), parts along dimension 0, may hold values from -6 to 6
- video_query_gain: float32 [2048], P('head'), may hold values from 1 to 2
- video_key_gain: float32 [2048], P('head'), may hold values from 1 to 2
- audio_query_gain: float32 [2048], P('head'), may hold values from 1 to 2
- audio_key_gain: float32 [2048], P('head'), may hold values from 1 to 2
Outputs:
- video_mixed: bfloat16 [2048, 2048], P(('clips', 'seq'), 'head'), parts along dimension 0
- audio_mixed: bfloat16 [512, 2048], P(('clips', 'seq'), 'head'), parts along dimension 0
There are 2 independent parts, one for each index of `clips`. A program takes and returns all parts, laid end to end along the dimension named above; an argument that names none is the same for every part. Nothing has to cross between parts.
All inputs are finite; a program needn't handle non-finite values.
Results may differ from a plain program's by a relative error of at most 0.02.
Values may be sent and summed in bfloat16 or wider, within the bound.
A program may use at most 128 MiB of HBM per device.

v0:
```python
import functools
import math

import jax
import jax.numpy as jnp
from jax import lax
from jax.experimental import pallas as pl
from jax.experimental.pallas import tpu as pltpu
from jax.sharding import PartitionSpec as P

HEAD_DIM = 128
EXP2_SCALE = HEAD_DIM ** (-0.5) * math.log2(math.e)


def normed(tokens, gain_row):
    count = tokens.shape[0]
    head_count = tokens.shape[1] // HEAD_DIM
    entries = tokens.astype(jnp.float32).reshape(count, head_count, HEAD_DIM)
    scaled = entries * lax.rsqrt(jnp.mean(entries * entries, axis=2, keepdims=True) + 1e-06)
    return (scaled.reshape(count, head_count * HEAD_DIM) * gain_row).astype(jnp.bfloat16)


def start_state(row_count, head_count):
    return (
        jnp.full((head_count, row_count), -1e30, jnp.float32),
        jnp.zeros((head_count, row_count), jnp.float32),
        jnp.zeros((row_count, head_count, HEAD_DIM), jnp.float32),
    )


def folding(queries, prepare):
    head_count = queries.shape[1]

    def fold_step(state_now, pieces, offset):
        key_rows, values = prepare(pieces)
        key_rows = key_rows.reshape(key_rows.shape[0], head_count, HEAD_DIM)
        values = values.reshape(values.shape[0], head_count, HEAD_DIM)
        scores = jnp.einsum(
            "qhd,khd->hqk", queries, key_rows, preferred_element_type=jnp.float32
        ) * HEAD_DIM ** (-0.5)
        running_max, row_total, accumulated = state_now
        new_max = jnp.maximum(running_max, jnp.max(scores, axis=2))
        rescale = jnp.exp(running_max - new_max)
        weights = jnp.exp(scores - new_max[:, :, None])
        row_total = jnp.sum(weights, axis=2)
        update = jnp.einsum(
            "hqk,khd->qhd", weights.astype(jnp.bfloat16), values, preferred_element_type=jnp.float32
        )
        accumulated = accumulated * rescale.T[:, :, None] + update
        return (new_max, row_total, accumulated)

    return fold_step


def finish(state_now):
    running_max, row_total, accumulated = state_now
    result = accumulated / row_total.T[:, :, None]
    return result.reshape(result.shape[0], result.shape[1] * HEAD_DIM)


def as_heads(tokens):
    return tokens.reshape(tokens.shape[0], tokens.shape[1] // HEAD_DIM, HEAD_DIM)


def keep_pair(pieces):
    return pieces


def per_device(
    video_q,
    video_k,
    video_v,
    audio_q,
    audio_k,
    audio_v,
    video_query_gain,
    video_key_gain,
    audio_query_gain,
    audio_key_gain,
):
    head_count = video_q.shape[1] // HEAD_DIM
    video_rows = video_q.shape[0]
    audio_rows = audio_q.shape[0]
    video_state = folding(as_heads(video_q), keep_pair)(
        start_state(video_rows, head_count),
        (
            lax.all_gather(video_k, "seq", axis=0, tiled=True),
            lax.all_gather(video_v, "seq", axis=0, tiled=True),
        ),
        jnp.int32(0),
    )
    video_self = finish(video_state).astype(jnp.bfloat16)
    audio_state = folding(as_heads(audio_q), keep_pair)(
        start_state(audio_rows, head_count),
        (
            lax.all_gather(audio_k, "seq", axis=0, tiled=True),
            lax.all_gather(audio_v, "seq", axis=0, tiled=True),
        ),
        jnp.int32(0),
    )
    audio_self = finish(audio_state).astype(jnp.bfloat16)
    audio_whole = lax.all_gather(audio_self, "seq", axis=0, tiled=True)
    video_queries = as_heads(normed(video_self, video_query_gain))
    cross_step = folding(video_queries, keep_pair)
    video_cross = finish(
        cross_step(
            start_state(video_rows, head_count),
            (normed(audio_whole, audio_key_gain), audio_whole),
            0,
        )
    )
    audio_queries = normed(audio_self, audio_query_gain)

    def prepare_video(shard_rows):
        return (normed(shard_rows, video_key_gain), shard_rows)

    audio_state_cross = folding(as_heads(audio_queries), prepare_video)(
        start_state(audio_rows, head_count),
        lax.all_gather(video_self, "seq", axis=0, tiled=True),
        jnp.int32(0),
    )
    audio_cross = finish(audio_state_cross)
    video_mixed = (video_self.astype(jnp.float32) + video_cross).astype(jnp.bfloat16)
    audio_mixed = (audio_self.astype(jnp.float32) + audio_cross).astype(jnp.bfloat16)
    return (video_mixed, audio_mixed)


def attend_kernel(
    n,
    video_q,
    video_k,
    video_v,
    audio_q,
    audio_k,
    audio_v,
    video_query_gain_in,
    video_key_gain_in,
    audio_query_gain_in,
    audio_key_gain_in,
    video_out,
    audio_out,
    vq,
    vk,
    vv,
    aq,
    ak,
    av,
    audio_self,
    audio_queries,
    audio_keys,
    audio_sum,
    video_mixed,
    audio_mixed,
    send_sem,
    recv_sem,
    own_sem,
    out_send_sem,
    out_recv_sem,
    out_own_sem,
    far_in_sem,
    video_query_gain,
    video_key_gain,
    audio_query_gain,
    audio_key_gain,
    gain_sem,
):
    me = lax.axis_index("seq")
    rows = video_q.shape[0]
    arows = audio_q.shape[0]

    half = n // 2 if n % 2 == 0 else n
    far_count = n - half

    def near_peer(step, sign):
        return me // half * half + lax.rem(lax.rem(me, half) + half + sign * step, half)

    def far_peer(step, sign):
        return lax.rem(near_peer(step, sign) + half, n)

    def over_peers(visit, sign, far_first):
        def far(step, carry):
            visit(far_peer(step, sign))
            return carry

        def near(step, carry):
            visit(near_peer(step, sign))
            return carry

        if far_first:
            lax.fori_loop(0, far_count, far, 0)
        lax.fori_loop(1, half, near, 0)
        if not far_first:
            lax.fori_loop(0, far_count, far, 0)

    def head_columns(index):
        return pl.ds(pl.multiple_of(index * HEAD_DIM, HEAD_DIM), HEAD_DIM)

    def token_rows(index, count):
        return pl.ds(pl.multiple_of(index * count, count), count)

    ins = (
        (audio_k, ak, arows),
        (audio_v, av, arows),
        (audio_q, aq, arows),
        (video_k, vk, rows),
        (video_v, vv, rows),
        (video_q, vq, rows),
    )

    def own_in(kind):
        source, target, count = ins[kind]
        return pltpu.make_async_copy(
            source.at[:, head_columns(me)],
            target.at[token_rows(me, count), pl.ds(0, HEAD_DIM)],
            own_sem.at[kind],
        )

    def sent_in(kind, peer):
        source, target, count = ins[kind]
        return pltpu.make_async_remote_copy(
            src_ref=source.at[:, head_columns(peer)],
            dst_ref=target.at[token_rows(me, count), pl.ds(0, HEAD_DIM)],
            send_sem=send_sem.at[kind, peer],
            recv_sem=recv_sem.at[kind, me],
            device_id={"seq": peer},
            device_id_type=pl.DeviceIdType.MESH,
        )

    def received_in(kind, peer):
        source, target, count = ins[kind]
        return pltpu.make_async_remote_copy(
            src_ref=source.at[:, head_columns(peer)],
            dst_ref=target.at[token_rows(peer, count), pl.ds(0, HEAD_DIM)],
            send_sem=send_sem.at[kind, peer],
            recv_sem=recv_sem.at[kind, peer],
            device_id={"seq": peer},
            device_id_type=pl.DeviceIdType.MESH,
        )

    outs = ((audio_mixed, audio_out, arows), (video_mixed, video_out, rows))

    def own_out(kind):
        source, target, count = outs[kind]
        return pltpu.make_async_copy(
            source.at[token_rows(me, count), :],
            target.at[:, head_columns(me)],
            out_own_sem.at[kind],
        )

    def sent_out(kind, peer):
        source, target, count = outs[kind]
        return pltpu.make_async_remote_copy(
            src_ref=source.at[token_rows(peer, count), :],
            dst_ref=target.at[:, head_columns(me)],
            send_sem=out_send_sem.at[kind, peer],
            recv_sem=out_recv_sem.at[kind, me],
            device_id={"seq": peer},
            device_id_type=pl.DeviceIdType.MESH,
        )

    def received_out(kind, peer):
        source, target, count = outs[kind]
        return pltpu.make_async_remote_copy(
            src_ref=source.at[token_rows(peer, count), :],
            dst_ref=target.at[:, head_columns(peer)],
            send_sem=out_send_sem.at[kind, peer],
            recv_sem=out_recv_sem.at[kind, peer],
            device_id={"seq": peer},
            device_id_type=pl.DeviceIdType.MESH,
        )

    def signal(semaphore, peer):
        pl.semaphore_signal(
            semaphore,
            inc=1,
            device_id={"seq": peer},
            device_id_type=pl.DeviceIdType.MESH,
        )

    def send(kinds, peers):
        for kind in kinds:
            for peer in peers:
                sent_in(kind, peer).start()

    barrier = pltpu.get_barrier_semaphore()
    near = [near_peer(step, 1) for step in range(1, half)]
    far = [far_peer(step, 1) for step in range(far_count)]
    for peer in far[:1] + near:
        signal(barrier, peer)
    pl.semaphore_wait(barrier, len(far[:1] + near))
    for peer in near:
        signal(far_in_sem, peer)
    for kinds, which in EARLY_ORDER:
        send(kinds, near if which == "near" else far[:1])
    if near:
        pl.semaphore_wait(far_in_sem, len(near))
    for kinds, which in LATE_ORDER:
        send(kinds, {"near": near, "rest": far[1:], "far": far}[which])

    gains = [
        pltpu.make_async_copy(source, target, gain_sem.at[index])
        for index, (source, target) in enumerate(
            (
                (video_query_gain_in, video_query_gain),
                (video_key_gain_in, video_key_gain),
                (audio_query_gain_in, audio_query_gain),
                (audio_key_gain_in, audio_key_gain),
            )
        )
    ]
    for gain in gains:
        gain.start()
    for kind in range(len(ins)):
        own_in(kind).start()

    ones = jnp.ones((arows * n, HEAD_DIM), jnp.bfloat16)
    av[:, HEAD_DIM:] = ones
    audio_self[:, HEAD_DIM:] = ones
    ones = jnp.ones((rows * n, HEAD_DIM), jnp.bfloat16)
    vv[:, HEAD_DIM:] = ones
    audio_sum[...] = jnp.zeros_like(audio_sum)

    def wait_kinds(kinds):
        for kind in kinds:
            own_in(kind).wait()

        def wait_peer(peer):
            for kind in kinds:
                received_in(kind, peer).wait_recv()

        over_peers(wait_peer, -1, False)

    def dot_t(left, right):
        return lax.dot_general(
            left, right, (((1,), (1,)), ((), ())), preferred_element_type=jnp.float32
        )

    def dot(left, right):
        return jnp.dot(left, right, preferred_element_type=jnp.float32)

    def self_attend(queries, key_rows, values):
        scores = dot_t(queries, key_rows)
        largest = jnp.max(scores, axis=1, keepdims=True)
        weights = jnp.exp2((scores - largest) * EXP2_SCALE).astype(jnp.bfloat16)
        both = dot(weights, values)
        return (both[:, :HEAD_DIM] / both[:, HEAD_DIM:]).astype(jnp.bfloat16)

    def unit(tokens):
        entries = tokens.astype(jnp.float32)
        mean = jnp.mean(entries * entries, axis=1, keepdims=True)
        return entries * lax.rsqrt(mean + 1e-06)

    own_head = pl.ds(me, 1)
    for gain in gains:
        gain.wait()
    wait_kinds((0, 1, 2))
    tokens = self_attend(aq[...], ak[...], av[...])
    audio_self[:, :HEAD_DIM] = tokens
    scaled = unit(tokens)
    audio_queries[...] = (scaled * audio_query_gain[own_head, :]).astype(jnp.bfloat16)
    audio_keys[...] = (scaled * audio_key_gain[own_head, :]).astype(jnp.bfloat16)

    wait_kinds((3, 4))

    def self_part(peers):
        here = [token_rows(peer, rows) for peer in peers]
        tokens = self_attend(jnp.concatenate([vq[one, :] for one in here], 0), vk[...], vv[...])
        scaled = unit(tokens)
        queries = (scaled * video_query_gain[own_head, :]).astype(jnp.bfloat16)
        key_rows = (scaled * video_key_gain[own_head, :]).astype(jnp.bfloat16)
        return tokens, queries, key_rows

    def audio_part(tokens, key_rows):
        weights = jnp.exp2(dot_t(audio_queries[...], key_rows) * EXP2_SCALE)
        values = jnp.concatenate([tokens, jnp.ones_like(tokens)], 1)
        audio_sum[...] += dot(weights.astype(jnp.bfloat16), values)

    def video_part(peers, tokens, queries):
        weights = jnp.exp2(dot_t(queries, audio_keys[...]) * EXP2_SCALE)
        both = dot(weights.astype(jnp.bfloat16), audio_self[...])
        cross = both[:, :HEAD_DIM] / both[:, HEAD_DIM:]
        mixed = (tokens.astype(jnp.float32) + cross).astype(jnp.bfloat16)
        for index, peer in enumerate(peers):
            video_mixed[token_rows(peer, rows), :] = mixed[index * rows : (index + 1) * rows]

    def send_audio(peer):
        sent_out(0, peer).start()

    others = [far_peer(step, -1) for step in range(far_count)]
    others += [near_peer(step, -1) for step in range(1, half)]
    group = GROUP if n % GROUP == 0 else 1
    for first in range(0, n, group):
        last = first + group == n
        here = others[first : first + group]
        for peer in here:
            received_in(5, peer).wait_recv()
        if last:
            own_in(5).wait()
        peers = here + [me] if last else here
        tokens, queries, key_rows = self_part(peers)
        if not last:
            video_part(peers, tokens, queries)
            for peer in here:
                sent_out(1, peer).start()
            audio_part(tokens, key_rows)
        else:
            audio_part(tokens, key_rows)
            both = audio_sum[...]
            cross = both[:, :HEAD_DIM] / both[:, HEAD_DIM:]
            audio_mixed[...] = (
                audio_self[:, :HEAD_DIM].astype(jnp.float32) + cross
            ).astype(jnp.bfloat16)
            own_out(0).start()
            over_peers(send_audio, 1, True)
            video_part(peers, tokens, queries)
            for peer in here:
                sent_out(1, peer).start()
            own_out(1).start()

    def finish_peer(peer):
        for kind in range(len(ins)):
            sent_in(kind, peer).wait_send()
        for kind in range(len(outs)):
            sent_out(kind, peer).wait_send()
            received_out(kind, peer).wait_recv()

    over_peers(finish_peer, 1, True)
    own_out(0).wait()
    own_out(1).wait()


def pass_on_kernel(video_in, audio_in, video_out, audio_out, sem):
    copies = (
        pltpu.make_async_copy(video_in, video_out, sem.at[0]),
        pltpu.make_async_copy(audio_in, audio_out, sem.at[1]),
    )
    for copy in copies:
        copy.start()
    for copy in copies:
        copy.wait()


GROUP = 2
KERNEL_BYTES = 24 * 2**20
EARLY_ORDER = (((0, 1, 2), "first"), ((0, 1, 2), "near"), ((3, 4), "first"), ((3, 4), "near"))
LATE_ORDER = (((0, 1, 2), "rest"), ((3, 4), "rest"), ((5,), "near"), ((5,), "far"))


def head_per_device(n, *arrays):
    video_q, audio_q = arrays[0], arrays[3]
    tokens, atokens = video_q.shape[0] * n, audio_q.shape[0] * n
    bf16, f32 = jnp.bfloat16, jnp.float32
    gains = [gain.reshape(n, HEAD_DIM) for gain in arrays[6:]]
    anywhere = pl.BlockSpec(memory_space=pl.ANY)
    operands = [
        pltpu.with_memory_space_constraint(one, pltpu.HBM) for one in (*arrays[:6], *gains)
    ]
    results = pl.pallas_call(
        functools.partial(attend_kernel, n),
        out_shape=(
            jax.ShapeDtypeStruct(video_q.shape, bf16),
            jax.ShapeDtypeStruct(audio_q.shape, bf16),
        ),
        in_specs=[anywhere] * 10,
        out_specs=(anywhere, anywhere),
        scratch_shapes=[
            pltpu.VMEM((tokens, HEAD_DIM), bf16),
            pltpu.VMEM((tokens, HEAD_DIM), bf16),
            pltpu.VMEM((tokens, 2 * HEAD_DIM), bf16),
            pltpu.VMEM((atokens, HEAD_DIM), bf16),
            pltpu.VMEM((atokens, HEAD_DIM), bf16),
            pltpu.VMEM((atokens, 2 * HEAD_DIM), bf16),
            pltpu.VMEM((atokens, 2 * HEAD_DIM), bf16),
            pltpu.VMEM((atokens, HEAD_DIM), bf16),
            pltpu.VMEM((atokens, HEAD_DIM), bf16),
            pltpu.VMEM((atokens, 2 * HEAD_DIM), f32),
            pltpu.VMEM((tokens, HEAD_DIM), bf16),
            pltpu.VMEM((atokens, HEAD_DIM), bf16),
            pltpu.SemaphoreType.DMA((6, n)),
            pltpu.SemaphoreType.DMA((6, n)),
            pltpu.SemaphoreType.DMA((6,)),
            pltpu.SemaphoreType.DMA((2, n)),
            pltpu.SemaphoreType.DMA((2, n)),
            pltpu.SemaphoreType.DMA((2,)),
            pltpu.SemaphoreType.REGULAR,
            *[pltpu.VMEM((n, HEAD_DIM), f32)] * 4,
            pltpu.SemaphoreType.DMA((4,)),
        ],
        compiler_params=pltpu.CompilerParams(
            collective_id=0, has_side_effects=True, vmem_limit_bytes=KERNEL_BYTES
        ),
    )(*operands)
    return pl.pallas_call(
        pass_on_kernel,
        out_shape=(
            jax.ShapeDtypeStruct(video_q.shape, bf16),
            jax.ShapeDtypeStruct(audio_q.shape, bf16),
        ),
        in_specs=[anywhere] * 2,
        out_specs=(anywhere, anywhere),
        scratch_shapes=[pltpu.SemaphoreType.DMA((2,))],
        compiler_params=pltpu.CompilerParams(vmem_limit_bytes=KERNEL_BYTES // 4),
    )(*results)


def solution(mesh):
    in_specs = (
        P(("clips", "seq"), "head"),
        P(("clips", "seq"), "head"),
        P(("clips", "seq"), "head"),
        P(("clips", "seq"), "head"),
        P(("clips", "seq"), "head"),
        P(("clips", "seq"), "head"),
        P("head"),
        P("head"),
        P("head"),
        P("head"),
    )
    out_specs = (P(("clips", "seq"), "head"), P(("clips", "seq"), "head"))
    sizes = dict(mesh.shape)

    def body(*arrays):
        video_q, audio_q = arrays[0], arrays[3]
        if (
            video_q.shape[1] == sizes["seq"] * HEAD_DIM
            and video_q.shape[0] % 16 == 0
            and audio_q.shape[0] % 16 == 0
        ):
            return head_per_device(sizes["seq"], *arrays)
        return per_device(*arrays)

    return jax.shard_map(
        body, mesh=mesh, in_specs=in_specs, out_specs=out_specs, check_vma=False
    )
```

profile of v0, /device:TPU:0, one launch (start us, length us, event | category | flops | bytes accessed | tf_op | source)
XLA Modules:
  0.0 39.1 jit_solution(4303016397021004794)
XLA Ops:
  0.6 37.7 %shard_map.113 = (bf16[128,1024]{1,0:T(8,128)(2,1)S(1)}, bf16[32,1024]{1,0:T(8,128)(2,1)S(1)}) custom-call(bf16[128,1024]{1,0:T(8,128)(2,1)} %video_q.1, bf16[128,1024]{1,0:T(8,128)(2,1)} %video_k.1, bf16[128,1024]{1,0:T(8,128)(2,1)} %video_v.1, bf16[32,1024]{1,0:T(8,128)(2,1)} %audio_q.1, bf16[32,1024]{1,0:T(8,128)(2,1)} %audio_k.1, ...), custom_call_target="tpu_custom_call" | custom-call | tf_op jit(solution)/shard_map/pallas_call | solution.py:458
  38.3 0.7 %shard_map.114 = (bf16[128,1024]{1,0:T(8,128)(2,1)}, bf16[32,1024]{1,0:T(8,128)(2,1)}) custom-call(bf16[128,1024]{1,0:T(8,128)(2,1)S(1)} %get-tuple-element.4.video_in, bf16[32,1024]{1,0:T(8,128)(2,1)S(1)} %get-tuple-element.5.audio_in), custom_call_target="tpu_custom_call" | custom-call | tf_op jit(solution)/shard_map/pallas_call | solution.py:493
where the time goes:
time: 39.3 us; the launch traced here: 39.1 us
  Pallas kernels  38.4 us (98%)
  between operations  0.64 us (2%)
    pallas_call x1, Pallas kernels, head_per_device(): pl.pallas_call(functools.partial(attend_kernel, n), out_shape=(jax.ShapeD...  37.7 us

commit v1 on v0

--- a/solution.py
+++ b/solution.py
@@ -157,7 +157,7 @@
     out_send_sem,
     out_recv_sem,
     out_own_sem,
-    far_in_sem,
+    in_sem,
     video_query_gain,
     video_key_gain,
     audio_query_gain,
@@ -168,29 +168,20 @@
     rows = video_q.shape[0]
     arows = audio_q.shape[0]
 
-    half = n // 2 if n % 2 == 0 else n
-    far_count = n - half
-
-    def near_peer(step, sign):
-        return me // half * half + lax.rem(lax.rem(me, half) + half + sign * step, half)
-
-    def far_peer(step, sign):
-        return lax.rem(near_peer(step, sign) + half, n)
-
-    def over_peers(visit, sign, far_first):
-        def far(step, carry):
-            visit(far_peer(step, sign))
-            return carry
-
-        def near(step, carry):
-            visit(near_peer(step, sign))
-            return carry
-
-        if far_first:
-            lax.fori_loop(0, far_count, far, 0)
-        lax.fori_loop(1, half, near, 0)
-        if not far_first:
-            lax.fori_loop(0, far_count, far, 0)
+    width = n // 4
+    place, lane = me // width, lax.rem(me, width)
+    middle = jnp.logical_or(place == 1, place == 2)
+    edge = jnp.logical_not(middle)
+    inner = lax.select(place < 2, 1, 2)
+    outer = lax.select(place < 2, 0, 3)
+
+    def device(column, step):
+        return column * width + lax.rem(lane + step, width)
+
+    mates = [device(place, step) for step in range(1, width)]
+    beside = [device(inner + outer - place, step) for step in range(width)]
+    far_middle = [device(3 - inner, step) for step in range(width)]
+    far_edge = [device(3 - outer, step) for step in range(width)]
 
     def head_columns(index):
         return pl.ds(pl.multiple_of(index * HEAD_DIM, HEAD_DIM), HEAD_DIM)
@@ -283,19 +274,95 @@
                 sent_in(kind, peer).start()
 
     barrier = pltpu.get_barrier_semaphore()
-    near = [near_peer(step, 1) for step in range(1, half)]
-    far = [far_peer(step, 1) for step in range(far_count)]
-    for peer in far[:1] + near:
-        signal(barrier, peer)
-    pl.semaphore_wait(barrier, len(far[:1] + near))
-    for peer in near:
-        signal(far_in_sem, peer)
-    for kinds, which in EARLY_ORDER:
-        send(kinds, near if which == "near" else far[:1])
-    if near:
-        pl.semaphore_wait(far_in_sem, len(near))
-    for kinds, which in LATE_ORDER:
-        send(kinds, {"near": near, "rest": far[1:], "far": far}[which])
+    first_lane = lane == 0
+    core = lax.axis_index("head")
+    leader = core == 0
+
+    def signal_core(semaphore):
+        pl.semaphore_signal(
+            semaphore,
+            inc=1,
+            device_id={"head": 1 - core},
+            device_id_type=pl.DeviceIdType.MESH,
+        )
+
+    def follow():
+        @pl.when(leader)
+        def _():
+            signal_core(in_sem.at[6])
+
+        @pl.when(jnp.logical_not(leader))
+        def _():
+            pl.semaphore_wait(in_sem.at[6], 1)
+
+    early, keys, queries_in = (0, 1, 2), (3, 4), (5,)
+
+    @pl.when(middle)
+    def _():
+        signal(barrier, far_middle[0])
+        signal(barrier, beside[0])
+
+        @pl.when(jnp.logical_not(leader))
+        def _():
+            signal_core(barrier)
+
+        pl.semaphore_wait(barrier, lax.select(first_lane, 1, 2) + lax.select(leader, 1, 0))
+
+        @pl.when(first_lane)
+        def _():
+            for peer in mates:
+                signal(barrier, peer)
+
+        send(early, far_middle[:1])
+        send(keys, far_middle[:1])
+
+        @pl.when(first_lane)
+        def _():
+            pl.semaphore_wait(in_sem.at[0], len(mates))
+
+        @pl.when(jnp.logical_not(first_lane))
+        def _():
+            signal(in_sem.at[0], me - lane)
+
+        send(early, far_middle[1:])
+        pl.semaphore_wait(in_sem.at[1], 1)
+        signal(in_sem.at[2], far_middle[0])
+        signal(in_sem.at[5], beside[0])
+        send(early, beside[:1] + mates)
+        pl.semaphore_wait(in_sem.at[2], 1)
+        for peer in mates:
+            signal(in_sem.at[3], peer)
+        send(early, far_edge[:1])
+        send(keys, far_edge[:1])
+        send(keys, beside[:1] + mates)
+        pl.semaphore_wait(in_sem.at[3], len(mates))
+        follow()
+        signal(in_sem.at[4], beside[0])
+        send(early, far_edge[1:] + beside[1:])
+        send(keys, far_edge[1:] + beside[1:])
+        send(keys, far_middle[1:])
+        send(queries_in, beside + mates)
+        send(queries_in, far_edge + far_middle)
+
+    @pl.when(edge)
+    def _():
+        @pl.when(jnp.logical_not(leader))
+        def _():
+            signal_core(barrier)
+
+        pl.semaphore_wait(barrier, lax.select(leader, 2, 1))
+        signal(in_sem.at[1], beside[0])
+        pl.semaphore_wait(in_sem.at[5], 1)
+        send(early, far_middle[:1] + beside[:1])
+        send(keys, far_middle[:1] + beside[:1])
+        pl.semaphore_wait(in_sem.at[4], 1)
+        follow()
+
+        send(early, far_edge + far_middle[1:])
+        send(keys, far_edge + far_middle[1:])
+        send(early, mates + beside[1:])
+        send(keys, mates + beside[1:])
+        send(queries_in, mates + beside)
 
     gains = [
         pltpu.make_async_copy(source, target, gain_sem.at[index])
@@ -320,15 +387,15 @@
     vv[:, HEAD_DIM:] = ones
     audio_sum[...] = jnp.zeros_like(audio_sum)
 
+    others = mates + beside + far_middle + far_edge
+
     def wait_kinds(kinds):
         for kind in kinds:
             own_in(kind).wait()
 
-        def wait_peer(peer):
+        for peer in others:
             for kind in kinds:
                 received_in(kind, peer).wait_recv()
-
-        over_peers(wait_peer, -1, False)
 
     def dot_t(left, right):
         return lax.dot_general(
@@ -362,6 +429,11 @@
 
     wait_kinds((3, 4))
 
+    @pl.when(edge)
+    def _():
+        send(queries_in, far_edge + far_middle)
+
+
     def self_part(peers):
         here = [token_rows(peer, rows) for peer in peers]
         tokens = self_attend(jnp.concatenate([vq[one, :] for one in here], 0), vk[...], vv[...])
@@ -383,27 +455,18 @@
         for index, peer in enumerate(peers):
             video_mixed[token_rows(peer, rows), :] = mixed[index * rows : (index + 1) * rows]
 
-    def send_audio(peer):
-        sent_out(0, peer).start()
-
-    others = [far_peer(step, -1) for step in range(far_count)]
-    others += [near_peer(step, -1) for step in range(1, half)]
-    group = GROUP if n % GROUP == 0 else 1
-    for first in range(0, n, group):
-        last = first + group == n
-        here = others[first : first + group]
-        for peer in here:
-            received_in(5, peer).wait_recv()
+    order = [me] + others
+    plan = ((0, 1), (2, 3), (6, 7), (4, 5))
+    for turn, members in enumerate(plan):
+        last = turn + 1 == len(plan)
+        peers = [order[index] for index in members]
+        for index, peer in zip(members, peers):
+            if index == 0:
+                own_in(5).wait()
+            else:
+                received_in(5, peer).wait_recv()
+        tokens, queries, key_rows = self_part(peers)
         if last:
-            own_in(5).wait()
-        peers = here + [me] if last else here
-        tokens, queries, key_rows = self_part(peers)
-        if not last:
-            video_part(peers, tokens, queries)
-            for peer in here:
-                sent_out(1, peer).start()
-            audio_part(tokens, key_rows)
-        else:
             audio_part(tokens, key_rows)
             both = audio_sum[...]
             cross = both[:, :HEAD_DIM] / both[:, HEAD_DIM:]
@@ -411,22 +474,27 @@
                 audio_self[:, :HEAD_DIM].astype(jnp.float32) + cross
             ).astype(jnp.bfloat16)
             own_out(0).start()
-            over_peers(send_audio, 1, True)
-            video_part(peers, tokens, queries)
-            for peer in here:
+            for peer in reversed(others):
+                sent_out(0, peer).start()
+        video_part(peers, tokens, queries)
+        for index, peer in zip(members, peers):
+            if index == 0:
+                own_out(1).start()
+            else:
                 sent_out(1, peer).start()
-            own_out(1).start()
-
-    def finish_peer(peer):
+        if not last:
+            audio_part(tokens, key_rows)
+
+    own_out(0).wait()
+    own_out(1).wait()
+    for peer in others:
         for kind in range(len(ins)):
             sent_in(kind, peer).wait_send()
         for kind in range(len(outs)):
             sent_out(kind, peer).wait_send()
+    for peer in others:
+        for kind in range(len(outs)):
             received_out(kind, peer).wait_recv()
-
-    over_peers(finish_peer, 1, True)
-    own_out(0).wait()
-    own_out(1).wait()
 
 
 def pass_on_kernel(video_in, audio_in, video_out, audio_out, sem):
@@ -442,8 +510,6 @@
 
 GROUP = 2
 KERNEL_BYTES = 24 * 2**20
-EARLY_ORDER = (((0, 1, 2), "first"), ((0, 1, 2), "near"), ((3, 4), "first"), ((3, 4), "near"))
-LATE_ORDER = (((0, 1, 2), "rest"), ((3, 4), "rest"), ((5,), "near"), ((5,), "far"))
 
 
 def head_per_device(n, *arrays):
@@ -482,7 +548,7 @@
             pltpu.SemaphoreType.DMA((2, n)),
             pltpu.SemaphoreType.DMA((2, n)),
             pltpu.SemaphoreType.DMA((2,)),
-            pltpu.SemaphoreType.REGULAR,
+            pltpu.SemaphoreType.REGULAR((7,)),
             *[pltpu.VMEM((n, HEAD_DIM), f32)] * 4,
             pltpu.SemaphoreType.DMA((4,)),
         ],
@@ -523,6 +589,7 @@
         video_q, audio_q = arrays[0], arrays[3]
         if (
             video_q.shape[1] == sizes["seq"] * HEAD_DIM
+            and sizes["seq"] == 8
             and video_q.shape[0] % 16 == 0
             and audio_q.shape[0] % 16 == 0
         ):

time: 39.3 us -> 36.4 us (0.926)
  Pallas kernels: 38.4 us -> 35.6 us
    pallas_call x1, Pallas kernels: 37.7 us -> 34.9 us  [head_per_device(): pl.pallas_call(functools.partial(attend_kernel, n), out_shape=(jax.ShapeD...]
where the time goes in v1:
time: 36.4 us; the launch traced here: 36.3 us
  Pallas kernels  35.6 us (98%)
  between operations  0.64 us (2%)
    pallas_call x1, Pallas kernels, head_per_device(): pl.pallas_call(functools.partial(attend_kernel, n), out_shape=(jax.ShapeD...  34.9 us
    pallas_call x1, Pallas kernels, head_per_device(): pl.pallas_call(pass_on_kernel, out_shape=(jax.ShapeDtypeStruct(video_q.sh...  0.74 us

profile of v1, /device:TPU:0, one launch (start us, length us, event | category | flops | bytes accessed | tf_op | source)
XLA Modules:
  0.0 36.3 jit_solution(17833810639247074182)
XLA Ops:
  0.6 34.9 %shard_map.113 = (bf16[128,1024]{1,0:T(8,128)(2,1)S(1)}, bf16[32,1024]{1,0:T(8,128)(2,1)S(1)}) custom-call(bf16[128,1024]{1,0:T(8,128)(2,1)} %video_q.1, bf16[128,1024]{1,0:T(8,128)(2,1)} %video_k.1, bf16[128,1024]{1,0:T(8,128)(2,1)} %video_v.1, bf16[32,1024]{1,0:T(8,128)(2,1)} %audio_q.1, bf16[32,1024]{1,0:T(8,128)(2,1)} %audio_k.1, ...), custom_call_target="tpu_custom_call" | custom-call | tf_op jit(solution)/shard_map/pallas_call | solution.py:524
  35.5 0.7 %shard_map.114 = (bf16[128,1024]{1,0:T(8,128)(2,1)}, bf16[32,1024]{1,0:T(8,128)(2,1)}) custom-call(bf16[128,1024]{1,0:T(8,128)(2,1)S(1)} %get-tuple-element.4.video_in, bf16[32,1024]{1,0:T(8,128)(2,1)S(1)} %get-tuple-element.5.audio_in), custom_call_target="tpu_custom_call" | custom-call | tf_op jit(solution)/shard_map/pallas_call | solution.py:559

commit v2 on v1

--- a/solution.py
+++ b/solution.py
@@ -153,15 +153,11 @@
     audio_mixed,
     send_sem,
     recv_sem,
-    own_sem,
+    query_sem,
     out_send_sem,
     out_recv_sem,
-    out_own_sem,
     in_sem,
-    video_query_gain,
-    video_key_gain,
-    audio_query_gain,
-    audio_key_gain,
+    all_gains,
     gain_sem,
 ):
     me = lax.axis_index("seq")
@@ -198,35 +194,45 @@
         (video_q, vq, rows),
     )
 
+    own_class, beside_class = 0, 1
+    far_class = lax.select(middle, 2, 3)
+    classes = ([me] + mates, beside, far_middle, far_edge)
+
+    def landing(kind, turn):
+        return query_sem.at[turn] if kind == 5 else recv_sem.at[kind]
+
     def own_in(kind):
         source, target, count = ins[kind]
         return pltpu.make_async_copy(
             source.at[:, head_columns(me)],
             target.at[token_rows(me, count), pl.ds(0, HEAD_DIM)],
-            own_sem.at[kind],
-        )
-
-    def sent_in(kind, peer):
+            landing(kind, own_class),
+        )
+
+    def sent_in(kind, peer, turn):
         source, target, count = ins[kind]
         return pltpu.make_async_remote_copy(
             src_ref=source.at[:, head_columns(peer)],
             dst_ref=target.at[token_rows(me, count), pl.ds(0, HEAD_DIM)],
-            send_sem=send_sem.at[kind, peer],
-            recv_sem=recv_sem.at[kind, me],
+            send_sem=send_sem.at[kind],
+            recv_sem=landing(kind, turn),
             device_id={"seq": peer},
             device_id_type=pl.DeviceIdType.MESH,
         )
 
-    def received_in(kind, peer):
+    def wait_bytes(ref, semaphore):
+        pltpu.make_async_copy(ref, ref, semaphore).wait()
+
+    def wait_in(kind):
+        wait_bytes(ins[kind][1].at[:, pl.ds(0, HEAD_DIM)], recv_sem.at[kind])
+
+    def wait_queries(turn):
+        wait_bytes(vq.at[pl.ds(0, width * rows), :], query_sem.at[turn])
+
+    def wait_sent_in(kind):
         source, target, count = ins[kind]
-        return pltpu.make_async_remote_copy(
-            src_ref=source.at[:, head_columns(peer)],
-            dst_ref=target.at[token_rows(peer, count), pl.ds(0, HEAD_DIM)],
-            send_sem=send_sem.at[kind, peer],
-            recv_sem=recv_sem.at[kind, peer],
-            device_id={"seq": peer},
-            device_id_type=pl.DeviceIdType.MESH,
-        )
+        sent = target.at[pl.ds(0, (n - 1) * count), pl.ds(0, HEAD_DIM)]
+        wait_bytes(sent, send_sem.at[kind])
 
     outs = ((audio_mixed, audio_out, arows), (video_mixed, video_out, rows))
 
@@ -235,7 +241,7 @@
         return pltpu.make_async_copy(
             source.at[token_rows(me, count), :],
             target.at[:, head_columns(me)],
-            out_own_sem.at[kind],
+            out_recv_sem.at[kind],
         )
 
     def sent_out(kind, peer):
@@ -243,22 +249,16 @@
         return pltpu.make_async_remote_copy(
             src_ref=source.at[token_rows(peer, count), :],
             dst_ref=target.at[:, head_columns(me)],
-            send_sem=out_send_sem.at[kind, peer],
-            recv_sem=out_recv_sem.at[kind, me],
+            send_sem=out_send_sem.at[kind],
+            recv_sem=out_recv_sem.at[kind],
             device_id={"seq": peer},
             device_id_type=pl.DeviceIdType.MESH,
         )
 
-    def received_out(kind, peer):
+    def wait_out(kind):
         source, target, count = outs[kind]
-        return pltpu.make_async_remote_copy(
-            src_ref=source.at[token_rows(peer, count), :],
-            dst_ref=target.at[:, head_columns(peer)],
-            send_sem=out_send_sem.at[kind, peer],
-            recv_sem=out_recv_sem.at[kind, peer],
-            device_id={"seq": peer},
-            device_id_type=pl.DeviceIdType.MESH,
-        )
+        wait_bytes(source.at[pl.ds(0, (n - 1) * count), :], out_send_sem.at[kind])
+        wait_bytes(target, out_recv_sem.at[kind])
 
     def signal(semaphore, peer):
         pl.semaphore_signal(
@@ -271,7 +271,11 @@
     def send(kinds, peers):
         for kind in kinds:
             for peer in peers:
-                sent_in(kind, peer).start()
+                sent_in(kind, peer, None).start()
+
+    def send_queries(peers, turn):
+        for peer in peers:
+            sent_in(5, peer, turn).start()
 
     barrier = pltpu.get_barrier_semaphore()
     first_lane = lane == 0
@@ -295,7 +299,7 @@
         def _():
             pl.semaphore_wait(in_sem.at[6], 1)
 
-    early, keys, queries_in = (0, 1, 2), (3, 4), (5,)
+    early, keys = (0, 1, 2), (3, 4)
 
     @pl.when(middle)
     def _():
@@ -341,8 +345,9 @@
         send(early, far_edge[1:] + beside[1:])
         send(keys, far_edge[1:] + beside[1:])
         send(keys, far_middle[1:])
-        send(queries_in, beside + mates)
-        send(queries_in, far_edge + far_middle)
+        send_queries(beside, beside_class)
+        send_queries(mates, own_class)
+        send_queries(far_edge + far_middle, far_class)
 
     @pl.when(edge)
     def _():
@@ -362,21 +367,17 @@
         send(keys, far_edge + far_middle[1:])
         send(early, mates + beside[1:])
         send(keys, mates + beside[1:])
-        send(queries_in, mates + beside)
-
-    gains = [
-        pltpu.make_async_copy(source, target, gain_sem.at[index])
-        for index, (source, target) in enumerate(
-            (
-                (video_query_gain_in, video_query_gain),
-                (video_key_gain_in, video_key_gain),
-                (audio_query_gain_in, audio_query_gain),
-                (audio_key_gain_in, audio_key_gain),
-            )
-        )
-    ]
-    for gain in gains:
-        gain.start()
+        send_queries(mates, own_class)
+        send_queries(beside, beside_class)
+
+    gains = (
+        video_query_gain_in,
+        video_key_gain_in,
+        audio_query_gain_in,
+        audio_key_gain_in,
+    )
+    for index, gain in enumerate(gains):
+        pltpu.make_async_copy(gain, all_gains.at[pl.ds(index * n, n), :], gain_sem).start()
     for kind in range(len(ins)):
         own_in(kind).start()
 
@@ -389,14 +390,6 @@
 
     others = mates + beside + far_middle + far_edge
 
-    def wait_kinds(kinds):
-        for kind in kinds:
-            own_in(kind).wait()
-
-        for peer in others:
-            for kind in kinds:
-                received_in(kind, peer).wait_recv()
-
     def dot_t(left, right):
         return lax.dot_general(
             left, right, (((1,), (1,)), ((), ())), preferred_element_type=jnp.float32
@@ -417,29 +410,32 @@
         mean = jnp.mean(entries * entries, axis=1, keepdims=True)
         return entries * lax.rsqrt(mean + 1e-06)
 
-    own_head = pl.ds(me, 1)
-    for gain in gains:
-        gain.wait()
-    wait_kinds((0, 1, 2))
+    def own_gain(index):
+        return all_gains[pl.ds(index * n + me, 1), :]
+
+    wait_bytes(all_gains, gain_sem)
+    for kind in early:
+        wait_in(kind)
     tokens = self_attend(aq[...], ak[...], av[...])
     audio_self[:, :HEAD_DIM] = tokens
     scaled = unit(tokens)
-    audio_queries[...] = (scaled * audio_query_gain[own_head, :]).astype(jnp.bfloat16)
-    audio_keys[...] = (scaled * audio_key_gain[own_head, :]).astype(jnp.bfloat16)
-
-    wait_kinds((3, 4))
+    audio_queries[...] = (scaled * own_gain(2)).astype(jnp.bfloat16)
+    audio_keys[...] = (scaled * own_gain(3)).astype(jnp.bfloat16)
+
+    for kind in keys:
+        wait_in(kind)
 
     @pl.when(edge)
     def _():
-        send(queries_in, far_edge + far_middle)
+        send_queries(far_edge + far_middle, far_class)
 
 
     def self_part(peers):
         here = [token_rows(peer, rows) for peer in peers]
         tokens = self_attend(jnp.concatenate([vq[one, :] for one in here], 0), vk[...], vv[...])
         scaled = unit(tokens)
-        queries = (scaled * video_query_gain[own_head, :]).astype(jnp.bfloat16)
-        key_rows = (scaled * video_key_gain[own_head, :]).astype(jnp.bfloat16)
+        queries = (scaled * own_gain(0)).astype(jnp.bfloat16)
+        key_rows = (scaled * own_gain(1)).astype(jnp.bfloat16)
         return tokens, queries, key_rows
 
     def audio_part(tokens, key_rows):
@@ -455,16 +451,11 @@
         for index, peer in enumerate(peers):
             video_mixed[token_rows(peer, rows), :] = mixed[index * rows : (index + 1) * rows]
 
-    order = [me] + others
-    plan = ((0, 1), (2, 3), (6, 7), (4, 5))
-    for turn, members in enumerate(plan):
-        last = turn + 1 == len(plan)
-        peers = [order[index] for index in members]
-        for index, peer in zip(members, peers):
-            if index == 0:
-                own_in(5).wait()
-            else:
-                received_in(5, peer).wait_recv()
+    turns = (0, 1, 3, 2)
+    for turn in turns:
+        last = turn == turns[-1]
+        peers = classes[turn]
+        wait_queries(turn)
         tokens, queries, key_rows = self_part(peers)
         if last:
             audio_part(tokens, key_rows)
@@ -477,24 +468,18 @@
             for peer in reversed(others):
                 sent_out(0, peer).start()
         video_part(peers, tokens, queries)
-        for index, peer in zip(members, peers):
-            if index == 0:
-                own_out(1).start()
-            else:
-                sent_out(1, peer).start()
+        if turn == own_class:
+            own_out(1).start()
+            peers = peers[1:]
+        for peer in peers:
+            sent_out(1, peer).start()
         if not last:
             audio_part(tokens, key_rows)
 
-    own_out(0).wait()
-    own_out(1).wait()
-    for peer in others:
-        for kind in range(len(ins)):
-            sent_in(kind, peer).wait_send()
-        for kind in range(len(outs)):
-            sent_out(kind, peer).wait_send()
-    for peer in others:
-        for kind in range(len(outs)):
-            received_out(kind, peer).wait_recv()
+    for kind in range(len(ins)):
+        wait_sent_in(kind)
+    for kind in range(len(outs)):
+        wait_out(kind)
 
 
 def pass_on_kernel(video_in, audio_in, video_out, audio_out, sem):
@@ -508,7 +493,6 @@
         copy.wait()
 
 
-GROUP = 2
 KERNEL_BYTES = 24 * 2**20
 
 
@@ -542,15 +526,14 @@
             pltpu.VMEM((atokens, 2 * HEAD_DIM), f32),
             pltpu.VMEM((tokens, HEAD_DIM), bf16),
             pltpu.VMEM((atokens, HEAD_DIM), bf16),
-            pltpu.SemaphoreType.DMA((6, n)),
-            pltpu.SemaphoreType.DMA((6, n)),
             pltpu.SemaphoreType.DMA((6,)),
-            pltpu.SemaphoreType.DMA((2, n)),
-            pltpu.SemaphoreType.DMA((2, n)),
+            pltpu.SemaphoreType.DMA((5,)),
+            pltpu.SemaphoreType.DMA((4,)),
+            pltpu.SemaphoreType.DMA((2,)),
             pltpu.SemaphoreType.DMA((2,)),
             pltpu.SemaphoreType.REGULAR((7,)),
-            *[pltpu.VMEM((n, HEAD_DIM), f32)] * 4,
-            pltpu.SemaphoreType.DMA((4,)),
+            pltpu.VMEM((4 * n, HEAD_DIM), f32),
+            pltpu.SemaphoreType.DMA,
         ],
         compiler_params=pltpu.CompilerParams(
             collective_id=0, has_side_effects=True, vmem_limit_bytes=KERNEL_BYTES

time: 36.4 us -> 35.4 us (0.973)
  Pallas kernels: 35.6 us -> 34.5 us
    pallas_call x1, Pallas kernels: 34.9 us -> 33.8 us  [head_per_device(): pl.pallas_call(functools.partial(attend_kernel, n), out_shape=(jax.ShapeD...]
where the time goes in v2:
time: 35.4 us; the launch traced here: 35.2 us
  Pallas kernels  34.5 us (97%)
  between operations  0.64 us (2%)
    pallas_call x1, Pallas kernels, head_per_device(): pl.pallas_call(functools.partial(attend_kernel, n), out_shape=(jax.ShapeD...  33.8 us
    pallas_call x1, Pallas kernels, head_per_device(): pl.pallas_call(pass_on_kernel, out_shape=(jax.ShapeDtypeStruct(video_q.sh...  0.74 us

profile of v2, /device:TPU:0, one launch (start us, length us, event | category | flops | bytes accessed | tf_op | source)
XLA Modules:
  0.0 35.2 jit_solution(7660682573349175886)
XLA Ops:
  0.6 33.8 %shard_map.113 = (bf16[128,1024]{1,0:T(8,128)(2,1)S(1)}, bf16[32,1024]{1,0:T(8,128)(2,1)S(1)}) custom-call(bf16[128,1024]{1,0:T(8,128)(2,1)} %video_q.1, bf16[128,1024]{1,0:T(8,128)(2,1)} %video_k.1, bf16[128,1024]{1,0:T(8,128)(2,1)} %video_v.1, bf16[32,1024]{1,0:T(8,128)(2,1)} %audio_q.1, bf16[32,1024]{1,0:T(8,128)(2,1)} %audio_k.1, ...), custom_call_target="tpu_custom_call" | custom-call | tf_op jit(solution)/shard_map/pallas_call | solution.py:508
  34.5 0.7 %shard_map.114 = (bf16[128,1024]{1,0:T(8,128)(2,1)}, bf16[32,1024]{1,0:T(8,128)(2,1)}) custom-call(bf16[128,1024]{1,0:T(8,128)(2,1)S(1)} %get-tuple-element.4.video_in, bf16[32,1024]{1,0:T(8,128)(2,1)S(1)} %get-tuple-element.5.audio_in), custom_call_target="tpu_custom_call" | custom-call | tf_op jit(solution)/shard_map/pallas_call | solution.py:542

commit v3 on v2

--- a/solution.py
+++ b/solution.py
@@ -194,9 +194,11 @@
         (video_q, vq, rows),
     )
 
-    own_class, beside_class = 0, 1
+    own_class, beside_class, edge_class = 0, 1, 3
     far_class = lax.select(middle, 2, 3)
-    classes = ([me] + mates, beside, far_middle, far_edge)
+    middle_line = [(3 - inner) * width + index for index in range(width)]
+    edge_line = [(3 - outer) * width + index for index in range(width)]
+    classes = ([me] + mates, beside, middle_line, edge_line)
 
     def landing(kind, turn):
         return query_sem.at[turn] if kind == 5 else recv_sem.at[kind]
@@ -465,12 +467,16 @@
                 audio_self[:, :HEAD_DIM].astype(jnp.float32) + cross
             ).astype(jnp.bfloat16)
             own_out(0).start()
-            for peer in reversed(others):
+            for peer in edge_line + middle_line + beside + mates:
                 sent_out(0, peer).start()
+            for peer in held:
+                sent_out(1, peer).start()
         video_part(peers, tokens, queries)
         if turn == own_class:
             own_out(1).start()
             peers = peers[1:]
+        if turn == edge_class:
+            peers, held = peers[:1], peers[1:]
         for peer in peers:
             sent_out(1, peer).start()
         if not last:

time: 35.4 us -> 35 us (0.989)
    pallas_call x1, Pallas kernels: 33.8 us -> 33.4 us  [head_per_device(): pl.pallas_call(functools.partial(attend_kernel, n), out_shape=(jax.ShapeD...]
where the time goes in v3:
time: 35 us; the launch traced here: 34.8 us
  Pallas kernels  34.2 us (98%)
  between operations  0.64 us (2%)
    pallas_call x1, Pallas kernels, head_per_device(): pl.pallas_call(functools.partial(attend_kernel, n), out_shape=(jax.ShapeD...  33.4 us
    pallas_call x1, Pallas kernels, head_per_device(): pl.pallas_call(pass_on_kernel, out_shape=(jax.ShapeDtypeStruct(video_q.sh...  0.74 us

profile of v3, /device:TPU:0, one launch (start us, length us, event | category | flops | bytes accessed | tf_op | source)
XLA Modules:
  0.0 34.8 jit_solution(5456224225048756898)
XLA Ops:
  0.6 33.4 %shard_map.113 = (bf16[128,1024]{1,0:T(8,128)(2,1)S(1)}, bf16[32,1024]{1,0:T(8,128)(2,1)S(1)}) custom-call(bf16[128,1024]{1,0:T(8,128)(2,1)} %video_q.1, bf16[128,1024]{1,0:T(8,128)(2,1)} %video_k.1, bf16[128,1024]{1,0:T(8,128)(2,1)} %video_v.1, bf16[32,1024]{1,0:T(8,128)(2,1)} %audio_q.1, bf16[32,1024]{1,0:T(8,128)(2,1)} %audio_k.1, ...), custom_call_target="tpu_custom_call" | custom-call | tf_op jit(solution)/shard_map/pallas_call | solution.py:514
  34.1 0.7 %shard_map.114 = (bf16[128,1024]{1,0:T(8,128)(2,1)}, bf16[32,1024]{1,0:T(8,128)(2,1)}) custom-call(bf16[128,1024]{1,0:T(8,128)(2,1)S(1)} %get-tuple-element.4.video_in, bf16[32,1024]{1,0:T(8,128)(2,1)S(1)} %get-tuple-element.5.audio_in), custom_call_target="tpu_custom_call" | custom-call | tf_op jit(solution)/shard_map/pallas_call | solution.py:548

commit v4 on v3

--- a/solution.py
+++ b/solution.py
@@ -164,7 +164,7 @@
     rows = video_q.shape[0]
     arows = audio_q.shape[0]
 
-    width = n // 4
+    width = n // PLACES
     place, lane = me // width, lax.rem(me, width)
     middle = jnp.logical_or(place == 1, place == 2)
     edge = jnp.logical_not(middle)
@@ -308,32 +308,38 @@
         signal(barrier, far_middle[0])
         signal(barrier, beside[0])
 
-        @pl.when(jnp.logical_not(leader))
-        def _():
-            signal_core(barrier)
-
-        pl.semaphore_wait(barrier, lax.select(first_lane, 1, 2) + lax.select(leader, 1, 0))
-
         @pl.when(first_lane)
         def _():
             for peer in mates:
                 signal(barrier, peer)
 
+
+        @pl.when(jnp.logical_not(leader))
+        def _():
+            signal_core(barrier)
+
+        pl.semaphore_wait(barrier, lax.select(first_lane, 1, 2) + lax.select(leader, 1, 0))
+
+        @pl.when(jnp.logical_not(first_lane))
+        def _():
+            signal(in_sem.at[7], far_middle[0])
+            signal(in_sem.at[0], me - lane)
+
         send(early, far_middle[:1])
         send(keys, far_middle[:1])
 
-        @pl.when(first_lane)
-        def _():
-            pl.semaphore_wait(in_sem.at[0], len(mates))
-
-        @pl.when(jnp.logical_not(first_lane))
-        def _():
-            signal(in_sem.at[0], me - lane)
-
-        send(early, far_middle[1:])
         pl.semaphore_wait(in_sem.at[1], 1)
         signal(in_sem.at[2], far_middle[0])
         signal(in_sem.at[5], beside[0])
+        @pl.when(first_lane)
+        def _():
+            pl.semaphore_wait(in_sem.at[0], len(mates))
+
+        @pl.when(jnp.logical_not(first_lane))
+        def _():
+            pl.semaphore_wait(in_sem.at[7], 1)
+
+        send(early, far_middle[1:])
         send(early, beside[:1] + mates)
         pl.semaphore_wait(in_sem.at[2], 1)
         for peer in mates:
@@ -467,10 +473,12 @@
                 audio_self[:, :HEAD_DIM].astype(jnp.float32) + cross
             ).astype(jnp.bfloat16)
             own_out(0).start()
-            for peer in edge_line + middle_line + beside + mates:
+            for peer in edge_line:
                 sent_out(0, peer).start()
             for peer in held:
                 sent_out(1, peer).start()
+            for peer in middle_line:
+                sent_out(0, peer).start()
         video_part(peers, tokens, queries)
         if turn == own_class:
             own_out(1).start()
@@ -479,6 +487,9 @@
             peers, held = peers[:1], peers[1:]
         for peer in peers:
             sent_out(1, peer).start()
+        if last:
+            for peer in beside + mates:
+                sent_out(0, peer).start()
         if not last:
             audio_part(tokens, key_rows)
 
@@ -499,6 +510,7 @@
         copy.wait()
 
 
+PLACES, LANES = 4, 2
 KERNEL_BYTES = 24 * 2**20
 
 
@@ -537,7 +549,7 @@
             pltpu.SemaphoreType.DMA((4,)),
             pltpu.SemaphoreType.DMA((2,)),
             pltpu.SemaphoreType.DMA((2,)),
-            pltpu.SemaphoreType.REGULAR((7,)),
+            pltpu.SemaphoreType.REGULAR((8,)),
             pltpu.VMEM((4 * n, HEAD_DIM), f32),
             pltpu.SemaphoreType.DMA,
         ],
@@ -578,7 +590,8 @@
         video_q, audio_q = arrays[0], arrays[3]
         if (
             video_q.shape[1] == sizes["seq"] * HEAD_DIM
-            and sizes["seq"] == 8
+            and sizes["seq"] == PLACES * LANES
+            and sizes["head"] == 2
             and video_q.shape[0] % 16 == 0
             and audio_q.shape[0] % 16 == 0
         ):

time: 35 us -> 35 us (level)
  no operation moved by 1% of the time
where the time goes in v4:
time: 35 us; the launch traced here: 34.8 us
  Pallas kernels  34.1 us (97%)
  between operations  0.64 us (2%)
    pallas_call x1, Pallas kernels, head_per_device(): pl.pallas_call(functools.partial(attend_kernel, n), out_shape=(jax.ShapeD...  33.4 us
    pallas_call x1, Pallas kernels, head_per_device(): pl.pallas_call(pass_on_kernel, out_shape=(jax.ShapeDtypeStruct(video_q.sh...  0.74 us

profile of v4, /device:TPU:0, one launch (start us, length us, event | category | flops | bytes accessed | tf_op | source)
XLA Modules:
  0.0 34.8 jit_solution(990756596233675890)
XLA Ops:
  0.6 33.4 %shard_map.113 = (bf16[128,1024]{1,0:T(8,128)(2,1)S(1)}, bf16[32,1024]{1,0:T(8,128)(2,1)S(1)}) custom-call(bf16[128,1024]{1,0:T(8,128)(2,1)} %video_q.1, bf16[128,1024]{1,0:T(8,128)(2,1)} %video_k.1, bf16[128,1024]{1,0:T(8,128)(2,1)} %video_v.1, bf16[32,1024]{1,0:T(8,128)(2,1)} %audio_q.1, bf16[32,1024]{1,0:T(8,128)(2,1)} %audio_k.1, ...), custom_call_target="tpu_custom_call" | custom-call | tf_op jit(solution)/shard_map/pallas_call | solution.py:526
  34.0 0.7 %shard_map.114 = (bf16[128,1024]{1,0:T(8,128)(2,1)}, bf16[32,1024]{1,0:T(8,128)(2,1)}) custom-call(bf16[128,1024]{1,0:T(8,128)(2,1)S(1)} %get-tuple-element.4.video_in, bf16[32,1024]{1,0:T(8,128)(2,1)S(1)} %get-tuple-element.5.audio_in), custom_call_target="tpu_custom_call" | custom-call | tf_op jit(solution)/shard_map/pallas_call | solution.py:560
